TPU v7x, 32 devices: a whole 2x2x4 slice. The times are simulated.
32 devices in a mesh: grp: 2 (over y), ep: 4 (over z), fs: 4 (over x, core).
Axes of the slice: x: 2, y: 2, z: 4, core: 2. Of those that a mesh axis runs over, the one named last changes fastest.
Arguments:
- tokens: bfloat16 [4096, 2048], P(('grp', 'ep', 'fs')), parts along dimension 0, may hold values from -6 to 6
- expert_ids: int32 [4096, 8], P(('grp', 'ep', 'fs')), parts along dimension 0, may hold values from 0 to 63, as said below
- gate_values: float32 [4096, 8], P(('grp', 'ep', 'fs')), parts along dimension 0, may hold values from 0.1 to 1
- w_gate: bfloat16 [64, 2048, 768], P('ep', None, 'fs'), may hold values from -0.125 to 0.125
- w_up: bfloat16 [64, 2048, 768], P('ep', None, 'fs'), may hold values from -0.125 to 0.125
- w_down: bfloat16 [64, 768, 2048], P('ep', 'fs'), may hold values from -0.21875 to 0.21875
Outputs:
- combined: bfloat16 [4096, 2048], P(('grp', 'ep', 'fs')), parts along dimension 0
There are 2 independent parts, one for each index of `grp`. A program takes and returns all parts, laid end to end along the dimension named above; an argument that names none is the same for every part. Nothing has to cross between parts.
Inputs may be any that keep to these rules, and one draw needn't show every extreme that they name: `expert_ids`: each row names 8 different experts. In each aligned block of 128 rows (the rows of one device) no expert is named by more than 24 rows, and the 16 experts held by one index of ep, the same for all blocks, are each named by exactly 24 rows of every block.
All inputs are finite; a program needn't handle non-finite values.
Results may differ from a plain program's by a relative error of at most 0.0058.
Values may be sent and summed in bfloat16 or wider, within the bound.
A program may use at most 384 MiB of HBM per device.

v0:
```python
import jax
import jax.numpy as jnp
from jax import lax
from jax.sharding import PartitionSpec as P

ECAP = 24


def on_device(tokens, expert_ids, gate_values, w_gate, w_up, w_down):
    row_count, model_width = tokens.shape
    top_count = expert_ids.shape[1]
    local_count = w_gate.shape[0]
    axes = ("ep", "fs")
    blocks = lax.axis_size("ep") * lax.axis_size("fs")
    packed = jnp.concatenate([expert_ids.astype(jnp.float32), gate_values], axis=1)
    all_tokens = lax.all_gather(tokens, axes, axis=0, tiled=False)
    all_packed = lax.all_gather(packed, axes, axis=0, tiled=False)
    ids = all_packed[:, :, :top_count].astype(jnp.int32)
    gates = all_packed[:, :, top_count:]
    mine = lax.axis_index("ep") * local_count + jnp.arange(local_count, dtype=jnp.int32)
    match = ids[:, :, :, None] == mine
    member = jnp.any(match, axis=2)
    weight = jnp.sum(jnp.where(match, gates[:, :, :, None], 0.0), axis=2)
    place = jnp.cumsum(member.astype(jnp.int32), axis=1) - 1
    place = jnp.where(member, place, -1)
    pick = place.transpose(0, 2, 1)[:, :, None, :] == jnp.arange(ECAP, dtype=jnp.int32)[:, None]
    slot_weight = jnp.sum(
        jnp.where(pick, weight.transpose(0, 2, 1)[:, :, None, :], 0.0), axis=3
    )
    pick = pick.astype(jnp.bfloat16)
    rows = jnp.einsum("best,btd->besd", pick, all_tokens)
    rows = rows.transpose(1, 0, 2, 3).reshape(local_count, blocks * ECAP, model_width)
    gate_part = jnp.einsum("erd,edf->erf", rows, w_gate, preferred_element_type=jnp.float32)
    up_part = jnp.einsum("erd,edf->erf", rows, w_up, preferred_element_type=jnp.float32)
    hidden = (jax.nn.silu(gate_part) * up_part).astype(jnp.bfloat16)
    results = jnp.einsum("erf,efd->erd", hidden, w_down, preferred_element_type=jnp.float32)
    results = results.reshape(local_count, blocks, ECAP, model_width)
    results = (results * slot_weight.transpose(1, 0, 2)[:, :, :, None]).astype(jnp.bfloat16)
    partial = jnp.einsum(
        "best,ebsd->btd", pick, results, preferred_element_type=jnp.float32
    ).astype(jnp.bfloat16)
    summed = lax.psum_scatter(
        partial.reshape(blocks * row_count, model_width), axes, scatter_dimension=0, tiled=True
    )
    return summed


def solution(mesh):
    placed = (
        P(("grp", "ep", "fs"), None),
        P(("grp", "ep", "fs"), None),
        P(("grp", "ep", "fs"), None),
        P("ep", None, "fs"),
        P("ep", None, "fs"),
        P("ep", "fs", None),
    )
    return jax.shard_map(
        on_device,
        mesh=mesh,
        in_specs=placed,
        out_specs=P(("grp", "ep", "fs"), None),
        check_vma=False,
    )
```

profile of v0, /device:TPU:0, one launch (start us, length us, event | category | flops | bytes accessed | tf_op | source)
XLA Modules:
  0.0 314.7 jit_solution(8313495716115595692)
XLA Ops:
  6.5 0.0 all-gather.4.cloned.1.call-start
  6.5 0.7 all-gather.4.cloned.1.call-update
  7.3 0.0 reduce-scatter.2.cloned.1.call-start
  7.3 0.7 convert_element_type.19
  8.0 0.7 pad_maximum_fusion
  8.7 23.9 %all-gather = f32[2048,16]{0,1:T(8,128)S(1)} all-gather(f32[128,16]{0,1:T(8,128)S(1)} %pad_maximum_fusion), channel_id=2, replica_groups=mesh['grp'=2,'ep'=4,'fs'=4] {'ep','fs'}, dimensions={0}, use_global_device_ids=true | all-gather | bytes 139264 | tf_op jit(solution)/shard_map/all_gather | solution.py:17
  32.7 0.2 compare_reduce_fusion
  32.9 0.6 copy.18
  33.5 0.5 copy.17
  34.0 23.6 %select_bitcast_fusion = s32[16,16,128]{1,0,2:T(8,128)S(1)} fusion(pred[16,128,16]{2,0,1:T(8,128)(4,1)S(1)} %copy.18, s32[16,128,16]{2,0,1:T(8,128)S(1)} %copy.17), kind=kOutput, calls=%fused_computation.17 | output fusion | flops 4227072 | bytes 294912 | tf_op jit(solution)/shard_map/jit(cumsum)/reduce_window_sum | solution.py:24
  57.6 0.4 copy.19
  58.0 0.2 fusion.12
  58.2 1.2 select_reduce_fusion
  59.4 27.9 %all-gather.4.cloned.1.call-done = bf16[2048,2048]{1,0:T(8,128)(2,1)} async-done(((bf16[128,2048]{1,0:T(8,128)(2,1)}), bf16[2048,2048]{1,0:T(8,128)(2,1)}) %all-gather.4.cloned.1.call-update) | async-done | bytes 8388624 | tf_op jit(solution)/shard_map/all_gather | solution.py:16
  87.3 14.5 %convolution_bitcast_fusion = bf16[16,16,24,2048]{3,2,0,1:T(8,128)(2,1)} fusion(bf16[16,128,2048,1]{2,1,3,0:T(8,128)(2,1)} %bitcast.40, s32[16,16,128]{2,1,0:T(8,128)S(1)} %copy.19), kind=kOutput, calls=%fused_computation.5 | convolution fusion | flops 3222011904 | bytes 33685504 | tf_op jit(solution)/shard_map/best,btd->besd/dot_general | solution.py:31
  101.9 21.0 %copy.20 = bf16[16,16,24,2048]{3,2,1,0:T(8,128)(2,1)} copy(bf16[16,16,24,2048]{3,2,0,1:T(8,128)(2,1)} %convolution_bitcast_fusion) | data formatting | bytes 50331648 | tf_op jit(solution)/shard_map/transpose | solution.py:32
  122.9 19.1 %fusion.15 = f32[16,384,192]{1,2,0:T(8,128)} fusion(bf16[16,384,2048]{2,1,0:T(8,128)(2,1)} %bitcast.38, bf16[16,2048,192]{1,2,0:T(8,128)(2,1)} %param.9), kind=kOutput, calls=%fused_computation.23 | convolution fusion | flops 4831838208 | bytes 42467328 | tf_op jit(solution)/shard_map/erd,edf->erf/dot_general | solution.py:33
  141.9 18.2 %multiply_convert_fusion.4 = bf16[16,384,192]{1,2,0:T(8,128)(2,1)S(1)} fusion(f32[16,384,192]{1,2,0:T(8,128)} %fusion.15, bf16[16,384,2048]{2,1,0:T(8,128)(2,1)} %bitcast.39, bf16[16,2048,192]{1,2,0:T(8,128)(2,1)} %param.10), kind=kOutput, calls=%fused_computation.6.clone.clone.1 | convolution fusion | flops 4838916096 | bytes 44826624 | tf_op jit(solution)/shard_map/erd,edf->erf/dot_general | solution.py:34
  160.2 23.3 %fusion.6 = f32[16,384,2048]{2,1,0:T(8,128)} fusion(bf16[16,192,2048]{2,1,0:T(8,128)(2,1)} %param.11, bf16[16,384,192]{1,2,0:T(8,128)(2,1)S(1)} %multiply_convert_fusion.4), kind=kOutput, calls=%fused_computation.9 | convolution fusion | flops 4831838208 | bytes 65273856 | tf_op jit(solution)/shard_map/erf,efd->erd/dot_general | solution.py:36
  183.5 21.4 %bitcast_convert_fusion = bf16[16,128,2048]{2,1,0:T(8,128)(2,1)} fusion(f32[16,16,24,2048]{3,2,1,0:T(8,128)} %bitcast.36, f32[16,16,24]{2,0,1:T(8,128)S(1)} %bitcast.41, s32[16,16,128]{2,1,0:T(8,128)S(1)} %copy.19), kind=kOutput, calls=%fused_computation.4 | convolution fusion | flops 3251372032 | bytes 58875904 | tf_op jit(solution)/shard_map/best,ebsd->btd/dot_general | solution.py:39
  204.8 0.0 reduce-scatter.2.cloned.1.call-update
  204.8 103.0 %reduce-scatter.2.cloned.1.call-done = bf16[128,2048]{1,0:T(8,128)(2,1)} async-done(((bf16[2048,2048]{1,0:T(8,128)(2,1)}), bf16[128,2048]{1,0:T(8,128)(2,1)}) %reduce-scatter.2.cloned.1.call-update) | async-done | bytes 524304 | tf_op jit(solution)/shard_map/reduce_scatter | solution.py:42
  (6 shorter events, 0.1 us)
Async XLA Ops:
  6.5 80.8 %all-gather.4.cloned.1.call-start = ((), (), s32[]{:S(2)}) async-start(), calls=%async_computation.2 | async-start | bytes 8912896 | tf_op jit(solution)/shard_map/all_gather | solution.py:16
  7.3 300.6 %reduce-scatter.2.cloned.1.call-start = ((), (), s32[]{:S(2)}) async-start(), calls=%async_computation.1 | async-start | bytes 8912896 | tf_op jit(solution)/shard_map/reduce_scatter | solution.py:42
Sparse Core Ops, SparseCore 0:
  9.5 77.7 all-gather.3
  205.0 102.8 reduce-scatter.1
where the time goes:
time: 315 us
  waiting for transfers between devices  132 us (42%)
  matrix products  96.5 us (31%)
  other arithmetic  26.6 us (8%)
  blocking collectives  23.9 us (8%)
  local copies, waits for them, and re-layouts  22.6 us (7%)
  between operations  13.5 us (4%)
    reduce_scatter x1, waiting for transfers between devices, on_device(): lax.psum_scatter(partial.reshape(blocks * row_count, model_width), axes,...  103 us
    all_gather x1, waiting for transfers between devices, on_device(): all_tokens = lax.all_gather(tokens, axes, axis=0, tiled=False)  27.9 us
    all_gather x1, blocking collectives, on_device(): all_packed = lax.all_gather(packed, axes, axis=0, tiled=False)  23.9 us
    another operation x1, other arithmetic, on_device(): place = jnp.cumsum(member.astype(jnp.int32), axis=1) - 1  23.6 us
    dot_general x1, matrix products, on_device(): jnp.einsum('erf,efd->erd', hidden, w_down, preferred_element_type=jnp.flo...  23.3 us
    dot_general x1, matrix products, on_device(): jnp.einsum('best,ebsd->btd', pick, results, preferred_element_type=jnp.fl...  21.4 us
    transpose x1, local copies, waits for them, and re-layouts, on_device(): rows.transpose(1, 0, 2, 3).reshape(local_count, blocks * ECAP, model_width)  21 us
    dot_general x1, matrix products, on_device(): jnp.einsum('erd,edf->erf', rows, w_gate, preferred_element_type=jnp.float32)  19.1 us
  transfers between devices with their start and end apart: 2, of which 2 were waited for; matrix products, arithmetic and copies ran while one was open for 9% of the time, Pallas kernels for 0%

commit v1 on v0

--- a/solution.py
+++ b/solution.py
@@ -1,9 +1,326 @@
+import functools
+
 import jax
 import jax.numpy as jnp
 from jax import lax
+from jax.experimental import pallas as pl
+from jax.experimental.pallas import tpu as pltpu
 from jax.sharding import PartitionSpec as P
 
 ECAP = 24
+CHUNK = 512
+WBUF = 3
+MESH = pl.DeviceIdType.MESH
+
+
+def fused_kernel(
+    tok_ref, meta_in, wg_hbm, wu_hbm, wd_hbm, out_ref,
+    hold, meta, rows, slotw, pick, pickt, wbuf, core_buf, x_buf, z_buf,
+    own_sem, w_sem, m_send, m_recv, z_send, z_recv, x_send, x_recv, c_send, c_recv,
+    r1_send, r1_recv, r2_send, r2_recv, r3_send, r3_recv,
+):
+    experts = wg_hbm.shape[0]
+    ff = wg_hbm.shape[1]
+    width = tok_ref.shape[1]
+    tok = tok_ref.shape[0]
+    pair_slots = 2 * ECAP
+    top = meta_in.shape[0] // 2
+    e_me = lax.axis_index("ep")
+    f_me = lax.axis_index("fs")
+    x_me = f_me // 2
+    c_me = lax.rem(f_me, 2)
+    b_me = e_me * 4 + f_me
+    f_xn = (1 - x_me) * 2 + c_me
+    f_cn = x_me * 2 + 1 - c_me
+
+    def remote(source, target, ssem, rsem, ep, fs):
+        return pltpu.make_async_remote_copy(
+            src_ref=source, dst_ref=target, send_sem=ssem, recv_sem=rsem,
+            device_id={"ep": ep, "fs": fs}, device_id_type=MESH,
+        )
+
+    def weight_copies(e, slot):
+        return [
+            pltpu.make_async_copy(w.at[e], wbuf.at[slot, i], w_sem.at[slot, i])
+            for i, w in enumerate((wg_hbm, wu_hbm, wd_hbm))
+        ]
+
+    own = pltpu.make_async_copy(tok_ref, hold.at[b_me], own_sem.at[0])
+    own_meta = pltpu.make_async_copy(meta_in, meta.at[b_me], own_sem.at[1])
+    own.start()
+    own_meta.start()
+    for e in range(WBUF):
+        for copy in weight_copies(e, e):
+            copy.start()
+
+    barrier = pltpu.get_barrier_semaphore()
+    for i in range(1, 16):
+        peer = lax.rem(b_me + i, 16)
+        pl.semaphore_signal(
+            barrier, inc=1, device_id={"ep": peer // 4, "fs": lax.rem(peer, 4)},
+            device_id_type=MESH,
+        )
+    pl.semaphore_wait(barrier, 15)
+
+    def z_copy(k):
+        return remote(
+            tok_ref, hold.at[b_me], z_send.at[k - 1], z_recv.at[k - 1],
+            lax.rem(e_me + k, 4), f_me,
+        )
+
+    def group(j):
+        return lax.rem(e_me + 4 - j, 4)
+
+    def x_copy(j):
+        block = hold.at[group(j) * 4 + f_me]
+        return remote(block, block, x_send.at[j], x_recv.at[j], e_me, f_xn)
+
+    def c_copy(j, other):
+        block = hold.at[group(j) * 4 + (f_xn if other else f_me)]
+        return remote(
+            block, block, c_send.at[j * 2 + other], c_recv.at[j * 2 + other], e_me, f_cn
+        )
+
+    def meta_copy(i):
+        peer = lax.rem(b_me + i, 16)
+        return remote(
+            meta_in, meta.at[b_me], m_send.at[i - 1], m_recv.at[i - 1],
+            peer // 4, lax.rem(peer, 4),
+        )
+
+    for i in range(1, 16):
+        meta_copy(i).start()
+    for k in (1, 2, 3):
+        z_copy(k).start()
+    own.wait()
+    own_meta.wait()
+    x_copy(0).start()
+    c_copy(0, 0).start()
+    for i in range(1, 16):
+        source = lax.rem(b_me + 16 - i, 16)
+        remote(
+            meta_in, meta.at[source], m_send.at[i - 1], m_recv.at[i - 1],
+            source // 4, lax.rem(source, 4),
+        ).wait_recv()
+
+    def dispatch(q, first):
+        ids_row = lax.broadcasted_iota(jnp.int32, (experts, tok), 0)
+        wanted = (ids_row + e_me * experts).astype(jnp.float32)
+        upper = (
+            lax.broadcasted_iota(jnp.int32, (tok, tok), 0)
+            <= lax.broadcasted_iota(jnp.int32, (tok, tok), 1)
+        ).astype(jnp.float32).astype(jnp.bfloat16)
+        places, weights = [], []
+        for half in range(2):
+            table = meta[first + half]
+            member = jnp.zeros((experts, tok), jnp.float32)
+            weight = jnp.zeros((experts, tok), jnp.float32)
+            for k in range(top):
+                same = table[k : k + 1, :] == wanted
+                member = jnp.where(same, 1.0, member)
+                weight = jnp.where(same, table[top + k : top + k + 1, :], weight)
+            count = jnp.dot(
+                member.astype(jnp.bfloat16), upper, preferred_element_type=jnp.float32
+            )
+            places.append(jnp.where(member > 0.5, count - 1.0 + half * ECAP, -1.0))
+            weights.append(weight)
+        place = jnp.concatenate(places, axis=1)
+        weight = jnp.concatenate(weights, axis=1)
+        slot = lax.broadcasted_iota(jnp.int32, (pair_slots, 2 * tok), 0).astype(jnp.float32)
+        base = pl.multiple_of(q * pair_slots, pair_slots)
+        for e in range(experts):
+            hit = place[e : e + 1, :] == slot
+            pick[e * pair_slots : (e + 1) * pair_slots, :] = jnp.where(hit, 1.0, 0.0)
+            value = jnp.sum(
+                jnp.where(hit, weight[e : e + 1, :], 0.0), axis=1, keepdims=True
+            )
+            slotw[e, pl.ds(base, pair_slots), :] = jnp.broadcast_to(value, (pair_slots, 128))
+        pickt[q] = jnp.transpose(pick[...]).astype(jnp.bfloat16)
+
+        def part(n, carry):
+            columns = pl.ds(pl.multiple_of(n * CHUNK, CHUNK), CHUNK)
+            block = hold[pl.ds(first, 2), :, columns].reshape(2 * tok, CHUNK)
+            got = jnp.dot(
+                pick[...].astype(jnp.bfloat16), block, preferred_element_type=jnp.float32
+            )
+            rows[:, pl.ds(base, pair_slots), columns] = got.astype(jnp.bfloat16).reshape(
+                experts, pair_slots, CHUNK
+            )
+            return carry
+
+        lax.fori_loop(0, width // CHUNK, part, 0)
+
+    def c_arrival(j, other):
+        f_from = (1 - x_me if other else x_me) * 2 + 1 - c_me
+        block = hold.at[group(j) * 4 + f_from]
+        return remote(
+            block, block, c_send.at[j * 2 + other], c_recv.at[j * 2 + other], e_me, f_cn
+        )
+
+    def gather_step(j, carry):
+        @pl.when(j > 0)
+        def _():
+            block = hold.at[group(j) * 4 + f_me]
+            remote(
+                tok_ref, block, z_send.at[j - 1], z_recv.at[j - 1], group(j), f_me
+            ).wait_recv()
+            x_copy(j).start()
+            c_copy(j, 0).start()
+
+        c_arrival(j, 0).wait_recv()
+        dispatch(2 * j, group(j) * 4 + x_me * 2)
+        block = hold.at[group(j) * 4 + f_xn]
+        remote(block, block, x_send.at[j], x_recv.at[j], e_me, f_xn).wait_recv()
+        c_copy(j, 1).start()
+        c_arrival(j, 1).wait_recv()
+        dispatch(2 * j + 1, group(j) * 4 + (1 - x_me) * 2)
+        return carry
+
+    lax.fori_loop(0, 4, gather_step, 0)
+    for i in range(1, 16):
+        meta_copy(i).wait_send()
+    for k in (1, 2, 3):
+        z_copy(k).wait_send()
+    for j in range(4):
+        x_copy(j).wait_send()
+        c_copy(j, 0).wait_send()
+        c_copy(j, 1).wait_send()
+
+    def expert_step(e, carry):
+        slot = lax.rem(e, WBUF)
+        for copy in weight_copies(e, slot):
+            copy.wait()
+        given = rows[e]
+        over = (((1,), (1,)), ((), ()))
+        gate = lax.dot_general(
+            given, wbuf[slot, 0], over, preferred_element_type=jnp.float32
+        )
+        up = lax.dot_general(given, wbuf[slot, 1], over, preferred_element_type=jnp.float32)
+        hidden = (gate / (1.0 + jnp.exp(-gate)) * up).astype(jnp.bfloat16)
+        scale = jnp.concatenate([slotw[e]] * (CHUNK // 128), axis=1)
+        for n in range(width // CHUNK):
+            columns = slice(n * CHUNK, (n + 1) * CHUNK)
+            result = jnp.dot(
+                hidden, wbuf[slot, 2, :, columns], preferred_element_type=jnp.float32
+            )
+            rows[e, :, columns] = (result * scale).astype(jnp.bfloat16)
+
+        @pl.when(e + WBUF < experts)
+        def _():
+            for copy in weight_copies(e + WBUF, slot):
+                copy.start()
+
+        return carry
+
+    lax.fori_loop(0, experts, expert_step, 0)
+
+    def combine(q):
+        base = pl.multiple_of(q * pair_slots, pair_slots)
+
+        def part(n, carry):
+            columns = pl.ds(pl.multiple_of(n * CHUNK, CHUNK), CHUNK)
+            block = rows[:, pl.ds(base, pair_slots), columns].reshape(
+                experts * pair_slots, CHUNK
+            )
+            got = jnp.dot(pickt[q], block, preferred_element_type=jnp.float32)
+            got = got.astype(jnp.bfloat16)
+            hold[2 * q + c_me, :, columns] = got[:tok]
+            hold[2 * q + 1 - c_me, :, columns] = got[tok:]
+            return carry
+
+        lax.fori_loop(0, width // CHUNK, part, 0)
+
+    def r1_copy(q):
+        return remote(
+            hold.at[2 * q + 1], core_buf.at[q], r1_send.at[q], r1_recv.at[q], e_me, f_cn
+        )
+
+    def r2_copy(j):
+        return remote(
+            hold.at[4 * j + 2], x_buf.at[j], r2_send.at[j], r2_recv.at[j], e_me, f_xn
+        )
+
+    def r3_copy(j):
+        return remote(
+            hold.at[4 * j], z_buf.at[j - 1], r3_send.at[j - 1], r3_recv.at[j - 1],
+            group(j), f_me,
+        )
+
+    def finish(j):
+        r1_copy(2 * j).wait_recv()
+        r2_copy(j).wait_recv()
+        return (
+            hold[4 * j].astype(jnp.float32)
+            + core_buf[2 * j].astype(jnp.float32)
+            + x_buf[j].astype(jnp.float32)
+        )
+
+    def scatter_step(s, carry):
+        j = lax.rem(s + 1, 4)
+        combine(2 * j + 1)
+        r1_copy(2 * j + 1).start()
+        combine(2 * j)
+        r1_copy(2 * j).start()
+        r1_copy(2 * j + 1).wait_recv()
+        hold[4 * j + 2] = (
+            hold[4 * j + 2].astype(jnp.float32) + core_buf[2 * j + 1].astype(jnp.float32)
+        ).astype(jnp.bfloat16)
+        r2_copy(j).start()
+
+        @pl.when(s > 0)
+        def _():
+            hold[4 * s] = finish(s).astype(jnp.bfloat16)
+            r3_copy(s).start()
+
+        return carry
+
+    lax.fori_loop(0, 4, scatter_step, 0)
+    total = finish(0)
+    for j in (1, 2, 3):
+        r3_copy(j).wait_recv()
+        total = total + z_buf[j - 1].astype(jnp.float32)
+    out_ref[...] = total.astype(jnp.bfloat16)
+    for q in range(8):
+        r1_copy(q).wait_send()
+    for j in range(4):
+        r2_copy(j).wait_send()
+    for j in (1, 2, 3):
+        r3_copy(j).wait_send()
+
+
+def on_device_fused(tokens, expert_ids, gate_values, w_gate, w_up, w_down):
+    tok, width = tokens.shape
+    experts, ff = w_down.shape[:2]
+    packed = jnp.concatenate([expert_ids.T.astype(jnp.float32), gate_values.T], axis=0)
+    bf16, f32 = jnp.bfloat16, jnp.float32
+    dma = pltpu.SemaphoreType.DMA
+    vmem = pl.BlockSpec(memory_space=pltpu.VMEM)
+    hbm = pl.BlockSpec(memory_space=pl.ANY)
+    slots = 16 * ECAP
+    return pl.pallas_call(
+        fused_kernel,
+        out_shape=jax.ShapeDtypeStruct((tok, width), bf16),
+        in_specs=[vmem, vmem, hbm, hbm, hbm],
+        out_specs=vmem,
+        scratch_shapes=[
+            pltpu.VMEM((16, tok, width), bf16),
+            pltpu.VMEM((16,) + packed.shape, f32),
+            pltpu.VMEM((experts, slots, width), bf16),
+            pltpu.VMEM((experts, slots, 128), f32),
+            pltpu.VMEM((experts * 2 * ECAP, 2 * tok), f32),
+            pltpu.VMEM((8, 2 * tok, experts * 2 * ECAP), bf16),
+            pltpu.VMEM((WBUF, 3, ff, width), bf16),
+            pltpu.VMEM((8, tok, width), bf16),
+            pltpu.VMEM((4, tok, width), bf16),
+            pltpu.VMEM((3, tok, width), bf16),
+            dma((2,)), dma((WBUF, 3)), dma((15,)), dma((15,)),
+            dma((3,)), dma((3,)), dma((4,)), dma((4,)), dma((8,)), dma((8,)),
+            dma((8,)), dma((8,)), dma((4,)), dma((4,)), dma((3,)), dma((3,)),
+        ],
+        compiler_params=pltpu.CompilerParams(
+            collective_id=0, has_side_effects=True, vmem_limit_bytes=63 * 1024 * 1024
+        ),
+    )(tokens, packed, w_gate.swapaxes(1, 2), w_up.swapaxes(1, 2), w_down)
 
 
 def on_device(tokens, expert_ids, gate_values, w_gate, w_up, w_down):
@@ -54,8 +371,9 @@
         P("ep", None, "fs"),
         P("ep", "fs", None),
     )
+    small = mesh.shape["ep"] == 4 and mesh.shape["fs"] == 4
     return jax.shard_map(
-        on_device,
+        on_device_fused if small else on_device,
         mesh=mesh,
         in_specs=placed,
         out_specs=P(("grp", "ep", "fs"), None),

time: 315 us -> 182 us (0.58)
  Pallas kernels: 0 us -> 178 us
  waiting for transfers between devices: 132 us -> 0 us
  matrix products: 96.5 us -> 0 us
  other arithmetic: 26.6 us -> 1.97 us
  blocking collectives: 23.9 us -> 0 us
  local copies, waits for them, and re-layouts: 22.6 us -> 1.88 us
  between operations: 13.5 us -> 0.01 us
    pallas_call x0 -> x1, Pallas kernels: none -> 178 us  [on_device_fused(): pl.pallas_call(fused_kernel, out_shape=jax.ShapeDtypeStruct((tok, width),...]
    reduce_scatter x1 -> x0, waiting for transfers between devices: 103 us -> none  [on_device(): lax.psum_scatter(partial.reshape(blocks * row_count, model_width), axes,...]
    dot_general x5 -> x0, matrix products: 96.5 us -> none  [the longest x1 23.3 us: on_device(): jnp.einsum('erf,efd->erd', hidden, w_down, preferred_element_type=jnp.flo...]
    all_gather x1 -> x0, waiting for transfers between devices: 27.9 us -> none  [on_device(): all_tokens = lax.all_gather(tokens, axes, axis=0, tiled=False)]
    all_gather x1 -> x0, blocking collectives: 23.9 us -> none  [on_device(): all_packed = lax.all_gather(packed, axes, axis=0, tiled=False)]
    another operation x1 -> x0, other arithmetic: 23.6 us -> none  [on_device(): place = jnp.cumsum(member.astype(jnp.int32), axis=1) - 1]
    transpose x1 -> x0, local copies, waits for them, and re-layouts: 21 us -> none  [on_device(): rows.transpose(1, 0, 2, 3).reshape(local_count, blocks * ECAP, model_width)]
  transfers between devices with their start and end apart: 2 -> 0, of which waited for: 2 -> 0; matrix products, arithmetic and copies ran while one was open for 9% -> 0% of each run, Pallas kernels for 0% -> 0%
where the time goes in v1:
time: 182 us
  Pallas kernels  178 us (98%)
  other arithmetic  1.97 us (1%)
  local copies, waits for them, and re-layouts  1.88 us (1%)
    pallas_call x1, Pallas kernels, on_device_fused(): pl.pallas_call(fused_kernel, out_shape=jax.ShapeDtypeStruct((tok, width),...  178 us

profile of v1, /device:TPU:0, one launch (start us, length us, event | category | flops | bytes accessed | tf_op | source)
XLA Modules:
  0.0 182.0 jit_solution(7127375859809607103)
XLA Ops:
  0.0 0.7 convert_bitcast_fusion
  0.7 1.3 pad_maximum_fusion.meta_in
  2.0 178.2 %shard_map.64 = bf16[128,2048]{1,0:T(8,128)(2,1)} custom-call(bf16[128,2048]{1,0:T(8,128)(2,1)} %tok_ref.1, f32[16,128]{1,0:T(8,128)} %pad_maximum_fusion.meta_in, bf16[16,192,2048]{2,1,0:T(8,128)(2,1)} %bitcast.5, bf16[16,192,2048]{2,1,0:T(8,128)(2,1)} %bitcast.6, bf16[16,192,2048]{2,1,0:T(8,128)(2,1)} %wd_hbm.1), custom_call_target="tpu_custom_call" | custom-call | tf_op jit(solution)/shard_map/pallas_call | solution.py:300
  180.1 1.9 %copy.8 = bf16[128,2048]{1,0:T(8,128)(2,1)} copy(bf16[128,2048]{1,0:T(8,128)(2,1)} %shard_map.64) | data formatting | bytes 1048576

commit v2 on v1

--- a/solution.py
+++ b/solution.py
@@ -1,5 +1,3 @@
-import functools
-
 import jax
 import jax.numpy as jnp
 from jax import lax
@@ -15,12 +13,11 @@
 
 def fused_kernel(
     tok_ref, meta_in, wg_hbm, wu_hbm, wd_hbm, out_ref,
-    hold, meta, rows, slotw, pick, pickt, wbuf, core_buf, x_buf, z_buf,
-    own_sem, w_sem, m_send, m_recv, z_send, z_recv, x_send, x_recv, c_send, c_recv,
+    hold, meta, rows, slotw, pick, pickt, wbuf, core_buf, x_buf, z_buf, done,
+    own_sem, w_sem, m_send, m_recv, up_send, down_send, z_recv, x_send, x_recv, c_send, c_recv,
     r1_send, r1_recv, r2_send, r2_recv, r3_send, r3_recv,
 ):
     experts = wg_hbm.shape[0]
-    ff = wg_hbm.shape[1]
     width = tok_ref.shape[1]
     tok = tok_ref.shape[0]
     pair_slots = 2 * ECAP
@@ -62,14 +59,25 @@
         )
     pl.semaphore_wait(barrier, 15)
 
-    def z_copy(k):
-        return remote(
-            tok_ref, hold.at[b_me], z_send.at[k - 1], z_recv.at[k - 1],
-            lax.rem(e_me + k, 4), f_me,
-        )
-
     def group(j):
-        return lax.rem(e_me + 4 - j, 4)
+        if isinstance(j, int) and j == 0:
+            return e_me
+        if j == 1:
+            return jnp.where(e_me == 0, 1, e_me - 1)
+        if j == 2:
+            return jnp.where(e_me == 0, 2, jnp.where(e_me == 3, 1, e_me + 1))
+        return jnp.where(e_me < 2, 3, 0)
+
+    def z_copy(ep, up):
+        block = hold.at[ep * 4 + f_me]
+        sems = up_send if up else down_send
+        return remote(
+            block, block, sems.at[ep], z_recv.at[ep], e_me + 1 if up else e_me - 1, f_me
+        )
+
+    def z_arrival(ep):
+        block = hold.at[ep * 4 + f_me]
+        return remote(block, block, up_send.at[ep], z_recv.at[ep], lax.rem(e_me + 1, 4), f_me)
 
     def x_copy(j):
         block = hold.at[group(j) * 4 + f_me]
@@ -90,10 +98,19 @@
 
     for i in range(1, 16):
         meta_copy(i).start()
-    for k in (1, 2, 3):
-        z_copy(k).start()
     own.wait()
     own_meta.wait()
+
+    def relay(ep, act):
+        @pl.when(jnp.logical_and(ep <= e_me, e_me < 3))
+        def _():
+            act(z_copy(ep, True))
+
+        @pl.when(jnp.logical_and(ep >= e_me, e_me > 0))
+        def _():
+            act(z_copy(ep, False))
+
+    relay(e_me, lambda copy: copy.start())
     x_copy(0).start()
     c_copy(0, 0).start()
     for i in range(1, 16):
@@ -134,7 +151,7 @@
             value = jnp.sum(
                 jnp.where(hit, weight[e : e + 1, :], 0.0), axis=1, keepdims=True
             )
-            slotw[e, pl.ds(base, pair_slots), :] = jnp.broadcast_to(value, (pair_slots, 128))
+            slotw[e, pl.ds(q % 4 * pair_slots, pair_slots), :] = jnp.broadcast_to(value, (pair_slots, 128))
         pickt[q] = jnp.transpose(pick[...]).astype(jnp.bfloat16)
 
         def part(n, carry):
@@ -157,40 +174,33 @@
             block, block, c_send.at[j * 2 + other], c_recv.at[j * 2 + other], e_me, f_cn
         )
 
-    def gather_step(j, carry):
-        @pl.when(j > 0)
-        def _():
-            block = hold.at[group(j) * 4 + f_me]
-            remote(
-                tok_ref, block, z_send.at[j - 1], z_recv.at[j - 1], group(j), f_me
-            ).wait_recv()
+    def pass_on(j):
+        if j > 0:
+            ep = group(j)
+            z_arrival(ep).wait_recv()
+            relay(ep, lambda copy: copy.start())
             x_copy(j).start()
             c_copy(j, 0).start()
 
-        c_arrival(j, 0).wait_recv()
-        dispatch(2 * j, group(j) * 4 + x_me * 2)
+    def pass_across(j):
         block = hold.at[group(j) * 4 + f_xn]
         remote(block, block, x_send.at[j], x_recv.at[j], e_me, f_xn).wait_recv()
         c_copy(j, 1).start()
-        c_arrival(j, 1).wait_recv()
-        dispatch(2 * j + 1, group(j) * 4 + (1 - x_me) * 2)
-        return carry
-
-    lax.fori_loop(0, 4, gather_step, 0)
-    for i in range(1, 16):
-        meta_copy(i).wait_send()
-    for k in (1, 2, 3):
-        z_copy(k).wait_send()
-    for j in range(4):
-        x_copy(j).wait_send()
-        c_copy(j, 0).wait_send()
-        c_copy(j, 1).wait_send()
-
-    def expert_step(e, carry):
-        slot = lax.rem(e, WBUF)
+
+    def take(j, other):
+        c_arrival(j, other).wait_recv()
+        f_base = (1 - x_me if other else x_me) * 2
+        dispatch(2 * j + other, group(j) * 4 + f_base)
+
+    half_rows = 4 * pair_slots
+
+    def expert_step(t, half):
+        e = lax.rem(t, experts)
+        slot = lax.rem(t, WBUF)
         for copy in weight_copies(e, slot):
             copy.wait()
-        given = rows[e]
+        part = slice(half * half_rows, (half + 1) * half_rows)
+        given = rows[e, part, :]
         over = (((1,), (1,)), ((), ()))
         gate = lax.dot_general(
             given, wbuf[slot, 0], over, preferred_element_type=jnp.float32
@@ -203,16 +213,19 @@
             result = jnp.dot(
                 hidden, wbuf[slot, 2, :, columns], preferred_element_type=jnp.float32
             )
-            rows[e, :, columns] = (result * scale).astype(jnp.bfloat16)
-
-        @pl.when(e + WBUF < experts)
+            rows[e, part, columns] = (result * scale).astype(jnp.bfloat16)
+
+        @pl.when(t + WBUF < 2 * experts)
         def _():
-            for copy in weight_copies(e + WBUF, slot):
+            for copy in weight_copies(lax.rem(t + WBUF, experts), slot):
                 copy.start()
 
-        return carry
-
-    lax.fori_loop(0, experts, expert_step, 0)
+    def run_experts(half, first, last):
+        def step(t, carry):
+            expert_step(t, half)
+            return carry
+
+        lax.fori_loop(half * experts + first, half * experts + last, step, 0)
 
     def combine(q):
         base = pl.multiple_of(q * pair_slots, pair_slots)
@@ -224,62 +237,99 @@
             )
             got = jnp.dot(pickt[q], block, preferred_element_type=jnp.float32)
             got = got.astype(jnp.bfloat16)
-            hold[2 * q + c_me, :, columns] = got[:tok]
-            hold[2 * q + 1 - c_me, :, columns] = got[tok:]
+            done[2 * q + c_me, :, columns] = got[:tok]
+            done[2 * q + 1 - c_me, :, columns] = got[tok:]
             return carry
 
         lax.fori_loop(0, width // CHUNK, part, 0)
 
     def r1_copy(q):
         return remote(
-            hold.at[2 * q + 1], core_buf.at[q], r1_send.at[q], r1_recv.at[q], e_me, f_cn
+            done.at[2 * q + 1], core_buf.at[q], r1_send.at[q], r1_recv.at[q], e_me, f_cn
         )
 
     def r2_copy(j):
         return remote(
-            hold.at[4 * j + 2], x_buf.at[j], r2_send.at[j], r2_recv.at[j], e_me, f_xn
+            done.at[4 * j + 2], x_buf.at[j], r2_send.at[j], r2_recv.at[j], e_me, f_xn
         )
 
     def r3_copy(j):
         return remote(
-            hold.at[4 * j], z_buf.at[j - 1], r3_send.at[j - 1], r3_recv.at[j - 1],
-            group(j), f_me,
+            done.at[4 * j], z_buf.at[lax.rem(e_me + 4 - group(j), 4) - 1], r3_send.at[j - 1], r3_recv.at[e_me], group(j), f_me,
         )
 
     def finish(j):
         r1_copy(2 * j).wait_recv()
         r2_copy(j).wait_recv()
         return (
-            hold[4 * j].astype(jnp.float32)
+            done[4 * j].astype(jnp.float32)
             + core_buf[2 * j].astype(jnp.float32)
             + x_buf[j].astype(jnp.float32)
         )
 
-    def scatter_step(s, carry):
-        j = lax.rem(s + 1, 4)
+    def emit(j):
         combine(2 * j + 1)
         r1_copy(2 * j + 1).start()
         combine(2 * j)
         r1_copy(2 * j).start()
+
+    def emit_across(j):
         r1_copy(2 * j + 1).wait_recv()
-        hold[4 * j + 2] = (
-            hold[4 * j + 2].astype(jnp.float32) + core_buf[2 * j + 1].astype(jnp.float32)
+        done[4 * j + 2] = (
+            done[4 * j + 2].astype(jnp.float32) + core_buf[2 * j + 1].astype(jnp.float32)
         ).astype(jnp.bfloat16)
         r2_copy(j).start()
 
-        @pl.when(s > 0)
-        def _():
-            hold[4 * s] = finish(s).astype(jnp.bfloat16)
-            r3_copy(s).start()
-
-        return carry
-
-    lax.fori_loop(0, 4, scatter_step, 0)
+    def emit_along(j):
+        done[4 * j] = finish(j).astype(jnp.bfloat16)
+        r3_copy(j).start()
+
+    quarter = experts // 4
+    take(0, 0)
+    pass_across(0)
+    pass_on(1)
+    take(0, 1)
+    take(1, 0)
+    pass_across(1)
+    pass_on(2)
+    take(1, 1)
+    run_experts(0, 0, quarter)
+    pass_across(2)
+    pass_on(3)
+    run_experts(0, quarter, 3 * quarter)
+    pass_across(3)
+    run_experts(0, 3 * quarter, experts)
+    emit(1)
+    emit(0)
+    emit_across(1)
+    emit_across(0)
+    for j in (2, 3):
+        take(j, 0)
+        take(j, 1)
+    run_experts(1, 0, 3 * quarter)
+    emit_along(1)
+    run_experts(1, 3 * quarter, experts)
+    emit(3)
+    emit_across(3)
+    emit(2)
+    emit_across(2)
+    emit_along(3)
+    emit_along(2)
     total = finish(0)
-    for j in (1, 2, 3):
-        r3_copy(j).wait_recv()
-        total = total + z_buf[j - 1].astype(jnp.float32)
+    for k in (1, 2, 3):
+        source = lax.rem(e_me + k, 4)
+        remote(
+            done.at[0], z_buf.at[k - 1], r3_send.at[0], r3_recv.at[source], source, f_me
+        ).wait_recv()
+        total = total + z_buf[k - 1].astype(jnp.float32)
     out_ref[...] = total.astype(jnp.bfloat16)
+    for i in range(1, 16):
+        meta_copy(i).wait_send()
+    for j in range(4):
+        relay(group(j), lambda copy: copy.wait_send())
+        x_copy(j).wait_send()
+        c_copy(j, 0).wait_send()
+        c_copy(j, 1).wait_send()
     for q in range(8):
         r1_copy(q).wait_send()
     for j in range(4):
@@ -300,22 +350,23 @@
     return pl.pallas_call(
         fused_kernel,
         out_shape=jax.ShapeDtypeStruct((tok, width), bf16),
-        in_specs=[vmem, vmem, hbm, hbm, hbm],
+        in_specs=[hbm, vmem, hbm, hbm, hbm],
         out_specs=vmem,
         scratch_shapes=[
             pltpu.VMEM((16, tok, width), bf16),
             pltpu.VMEM((16,) + packed.shape, f32),
             pltpu.VMEM((experts, slots, width), bf16),
-            pltpu.VMEM((experts, slots, 128), f32),
+            pltpu.VMEM((experts, slots // 2, 128), f32),
             pltpu.VMEM((experts * 2 * ECAP, 2 * tok), f32),
             pltpu.VMEM((8, 2 * tok, experts * 2 * ECAP), bf16),
             pltpu.VMEM((WBUF, 3, ff, width), bf16),
             pltpu.VMEM((8, tok, width), bf16),
             pltpu.VMEM((4, tok, width), bf16),
             pltpu.VMEM((3, tok, width), bf16),
+            pltpu.VMEM((16, tok, width), bf16),
             dma((2,)), dma((WBUF, 3)), dma((15,)), dma((15,)),
-            dma((3,)), dma((3,)), dma((4,)), dma((4,)), dma((8,)), dma((8,)),
-            dma((8,)), dma((8,)), dma((4,)), dma((4,)), dma((3,)), dma((3,)),
+            dma((4,)), dma((4,)), dma((4,)), dma((4,)), dma((4,)), dma((8,)), dma((8,)),
+            dma((8,)), dma((8,)), dma((4,)), dma((4,)), dma((3,)), dma((4,)),
         ],
         compiler_params=pltpu.CompilerParams(
             collective_id=0, has_side_effects=True, vmem_limit_bytes=63 * 1024 * 1024

time: 182 us -> 158 us (0.87)
  the two profiles are of different devices: /device:TPU:0 before, /device:TPU:17 now
where the time goes in v2:
time: 158 us
  Pallas kernels  154 us (97%)
  other arithmetic  1.97 us (1%)
  local copies, waits for them, and re-layouts  1.88 us (1%)
    pallas_call x1, Pallas kernels, on_device_fused(): pl.pallas_call(fused_kernel, out_shape=jax.ShapeDtypeStruct((tok, width),...  154 us

profile of v2, /device:TPU:17, one launch (start us, length us, event | category | flops | bytes accessed | tf_op | source)
XLA Modules:
  0.0 157.8 jit_solution(500778532573163788)
XLA Ops:
  0.0 0.7 convert_bitcast_fusion
  0.7 1.3 pad_maximum_fusion.meta_in
  2.0 153.9 %shard_map.64 = bf16[128,2048]{1,0:T(8,128)(2,1)} custom-call(bf16[128,2048]{1,0:T(8,128)(2,1)} %tok_ref.1, f32[16,128]{1,0:T(8,128)} %pad_maximum_fusion.meta_in, bf16[16,192,2048]{2,1,0:T(8,128)(2,1)} %bitcast.5, bf16[16,192,2048]{2,1,0:T(8,128)(2,1)} %bitcast.6, bf16[16,192,2048]{2,1,0:T(8,128)(2,1)} %wd_hbm.1), custom_call_target="tpu_custom_call" | custom-call | tf_op jit(solution)/shard_map/pallas_call | solution.py:350
  155.9 1.9 %copy.8 = bf16[128,2048]{1,0:T(8,128)(2,1)} copy(bf16[128,2048]{1,0:T(8,128)(2,1)} %shard_map.64) | data formatting | bytes 1048576
